TPU v7x, 32 devices: a whole 2x2x4 slice. The times are simulated.
32 devices in a mesh: group: 2 (over core), local: 16 (over z, y, x).
Axes of the slice: x: 2, y: 2, z: 4, core: 2. Of those that a mesh axis runs over, the one named last changes fastest.
Arguments:
- features: bfloat16 [64, 32, 1728], P(('group', 'local')), may hold values from -6 to 6
- neighbours: int32 [64, 27], P(('group', 'local')), may hold values from -1 to 1, as said below
- coarse_dest: int32 [64], P(('group', 'local')), may hold values from -1 to 3, as said below
- weight_first: bfloat16 [32, 864], replicated, may hold values from -0.21875 to 0.21875
- bias_first: float32 [32], replicated, may hold values from -3 to 3
- reduce_weight: bfloat16 [64, 256], replicated, may hold values from -0.375 to 0.375
- reduce_bias: float32 [64], replicated, may hold values from -3 to 3
- weight_coarse: bfloat16 [64, 1728], replicated, may hold values from -0.15625 to 0.15625
- bias_coarse: float32 [64], replicated, may hold values from -3 to 3
- weight_up: bfloat16 [32, 64], replicated, may hold values from -0.75 to 0.75
- bias_up: float32 [32], replicated, may hold values from -3 to 3
- weight_last: bfloat16 [32, 1728], replicated, may hold values from -0.15625 to 0.15625
- bias_last: float32 [32], replicated, may hold values from -3 to 3
Outputs:
- decoded: bfloat16 [64, 32, 1728], P(('group', 'local'))
- balanced_coarse: bfloat16 [128, 64, 216], P(('group', 'local'))
Inputs may be any that keep to these rules, and one draw needn't show every extreme that they name: `neighbours`: both slots of every device are live. For a live slot, entry (dx + 1) * 9 + (dy + 1) * 3 + dz + 1 names the live slot of the device with the same group index and local index l + dx that holds the block at offset (dx, dy, dz), or -1 where that block is absent or lies outside the group; entry 13 is the slot itself. The blocks of one device form one layer of blocks along the first dimension, the next local index holding the next layer. `coarse_dest`: -1 exactly for empty slots; else r * 2 + k, naming slot k of the coarse cubes that this device sends to the device of the same local index in group r. No two slots of a device share a value; in every draw some device sends 2 cubes to one group.
All inputs are finite; a program needn't handle non-finite values.
Results may differ from a plain program's by a relative error of at most 0.0049.
Values may be sent and summed in bfloat16 or wider, within the bound.
A program may use at most 64 MiB of HBM per device.

v0:
```python
import functools

import jax
import jax.numpy as jnp
from jax import lax
from jax.experimental import pallas as pl
from jax.experimental.pallas import tpu as pltpu
from jax.sharding import PartitionSpec as P

SEND_CAP = 2
MESH = pl.DeviceIdType.MESH
F32 = jnp.float32
BF16 = jnp.bfloat16
I32 = jnp.int32


def iota(shape, dim):
    return lax.broadcasted_iota(I32, shape, dim)


def onehot(mask):
    return jnp.where(mask, 1.0, 0.0).astype(BF16)


def column(row):
    n = row.shape[1]
    wide = jnp.broadcast_to(row, (n, n))
    return jnp.sum(jnp.where(iota((n, n), 0) == iota((n, n), 1), wide, 0.0), axis=1, keepdims=True)


def silu(u):
    return u / (1.0 + jnp.exp(-u))


def shifted(v, s):
    if s == 0:
        return v
    return jnp.concatenate([v[:, s:], v[:, :s]], axis=1)


def dot(a, b):
    return jnp.dot(a, b, preferred_element_type=F32)


def kernel(
    sizes,
    nb,
    dest,
    x_ref,
    w1_ref,
    b1_ref,
    wr_ref,
    br_ref,
    wc_ref,
    bc_ref,
    wu_ref,
    bu_ref,
    w2_ref,
    b2_ref,
    out_ref,
    bal_ref,
    sx,
    rx,
    sc,
    rc,
    sf,
    rf,
    su,
    ru,
    sb,
    rb,
    t1,
    t2,
    tred,
    tc,
    tup,
    tout,
    tbal,
    w1,
    wc,
    w2f,
    w2u,
    lhs,
    pad,
    y1,
    y2,
    fst,
    cin,
    up,
    red,
    send_sem,
    recv_sem,
    bal_send,
    bal_recv,
):
    side, count, ch, cc, n_local, n_group = sizes
    half = side // 2
    face = side * side
    planes = side + 2
    me = lax.axis_index("local")
    grp = lax.axis_index("group")
    right, left = lax.rem(me + 1, n_local), lax.rem(me + n_local - 1, n_local)
    ends = (left, right)

    def exchange(e, src, dst):
        copies = []
        for d in (0, 1):
            copies.append(
                pltpu.make_async_remote_copy(
                    src_ref=src.at[d],
                    dst_ref=dst.at[d],
                    send_sem=send_sem.at[e, d],
                    recv_sem=recv_sem.at[e, d],
                    device_id={"local": ends[d]},
                    device_id_type=MESH,
                )
            )
        return copies

    barrier = pltpu.get_barrier_semaphore()
    for e in ends:
        pl.semaphore_signal(barrier, inc=1, device_id={"local": e}, device_id_type=MESH)
    for d in range(1, n_group):
        pl.semaphore_signal(
            barrier, inc=1, device_id={"group": lax.rem(grp + d, n_group)}, device_id_type=MESH
        )
    for t in range(count):
        sx[0, t] = x_ref[t, :, 0:face]
        sx[1, t] = x_ref[t, :, (side - 1) * face : side * face]
    pl.semaphore_wait(barrier, 2 + n_group - 1)
    ex = exchange(0, sx, rx)
    for c in ex:
        c.start()

    n = iota((1, 256), 1)
    ny, nz = n >> 4, n & 15
    py = jnp.where(ny == 0, side - 1, jnp.where(ny == side + 1, 0, ny - 1))
    pz = jnp.where(nz == 0, side - 1, jnp.where(nz == side + 1, 0, nz - 1))
    inside = (ny < planes) & (nz < planes)
    t1[...] = onehot(iota((face, 256), 0) == jnp.where(inside, py * side + pz, -1))
    t2[...] = onehot(iota((256, 256), 0) == jnp.where(inside, py * 16 + pz, -1))
    n2 = iota((1, 512), 1)
    uy, uz = (n2 >> 4) & 15, n2 & 15
    qy = jnp.where(uy == 0, side - 1, jnp.where(uy == side + 1, 0, uy - 1))
    qz = jnp.where(uz == 0, side - 1, jnp.where(uz == side + 1, 0, uz - 1))
    target = (n2 >> 8) * 64 + (qy >> 1) * 8 + (qz >> 1)
    target = jnp.where((uy < planes) & (uz < planes), target, -1)
    tup[...] = onehot(iota((128, 512), 0) == target)
    ry, rz = (n2 >> 3) & 7, n2 & 7
    target = ((n2 >> 6) & 1) * 256 + (2 * ry + ((n2 >> 8) & 1)) * 16 + 2 * rz + ((n2 >> 7) & 1)
    target = jnp.where((ry < half) & (rz < half), target, -1)
    tred[...] = onehot(iota((512, 512), 0) == target)
    n1 = iota((1, 128), 1)
    cy, cz = (n1 >> 3) & 7, n1 & 7
    sy = jnp.where(cy == 0, half - 1, jnp.where(cy == half + 1, 0, cy - 1))
    sz = jnp.where(cz == 0, half - 1, jnp.where(cz == half + 1, 0, cz - 1))
    target = (n1 >> 6) * 64 + sy * 8 + sz
    tc[...] = onehot(iota((128, 128), 0) == target)
    k = iota((256, 1), 0)
    ky, kz = k >> 4, k & 15
    target = jnp.where((ky < side) & (kz < side), ky * side + kz, -1)
    tout[...] = onehot(iota((256, face), 1) == target)
    k = iota((64 * half, 1), 0)
    kx, ky, kz = k >> 6, (k >> 3) & 7, k & 7
    target = jnp.where((ky < half) & (kz < half), (kx * half + ky) * half + kz, -1)
    tbal[...] = onehot(iota((64 * half, half**3), 1) == target)

    for p in range(3):
        w1[p * ch : (p + 1) * ch] = w1_ref[:, p * 9 * ch : (p + 1) * 9 * ch]
        wc[p * cc : (p + 1) * cc] = wc_ref[:, p * 9 * cc : (p + 1) * 9 * cc]
        for part, dst in ((0, w2f), (1, w2u)):
            dst[p * ch : (p + 1) * ch] = jnp.concatenate(
                [
                    w2_ref[:, ((9 * p + k) * 2 + part) * ch : ((9 * p + k) * 2 + part + 1) * ch]
                    for k in range(9)
                ],
                axis=1,
            )
    b1, br, bc = column(b1_ref[...]), column(br_ref[...]), column(bc_ref[...])
    bu, b2 = column(bu_ref[...]), column(b2_ref[...])

    live = [jnp.where(nb[b, 13] >= 0, 1.0, 0.0) for b in range(count)]
    valid = [jnp.where(dest[b] >= 0, live[b], 0.0) for b in range(count)]

    def slot_row(b, step, dy, dz):
        row = jnp.zeros_like(dy)
        for iy in (-1, 0, 1):
            for iz in (-1, 0, 1):
                entry = nb[b, (step + 1) * 9 + (iy + 1) * 3 + iz + 1]
                row = jnp.where((dy == iy) & (dz == iz), entry, row)
        return row

    def as_masks(row):
        return [jnp.where(row == t, 1.0, 0.0) for t in range(count)]

    def offset(v, top):
        return jnp.where(v == 0, -1, jnp.where(v == top, 1, 0))

    fy, fz = offset(ny, side + 1), offset(nz, side + 1)
    gy, gz = offset(cy, half + 1), offset(cz, half + 1)
    fine = [[as_masks(slot_row(b, s, fy, fz)) for s in (-1, 0, 1)] for b in range(count)]
    mid = [as_masks(slot_row(b, 0, gy, gz)) for b in range(count)]
    rim = [
        as_masks(jnp.where(n1 < 64, slot_row(b, 1, gy, gz), slot_row(b, -1, gy, gz)))
        for b in range(count)
    ]

    def blend(parts, masks):
        total = parts[0] * masks[0]
        for part, mask in zip(parts[1:], masks[1:]):
            total = total + part * mask
        return total.astype(BF16)

    def taps(v, stride):
        return jnp.concatenate([shifted(v, q * stride + r) for q in range(3) for r in range(3)], axis=0)

    for t in range(count):
        for x in range(side):
            lhs[(x * count + t) * ch : (x * count + t + 1) * ch, 0:face] = x_ref[
                t, :, x * face : (x + 1) * face
            ]
    for x in range(side):
        a = dot(lhs[x * count * ch : (x + 1) * count * ch, 0:face], t1[...])
        parts = [a[t * ch : (t + 1) * ch] for t in range(count)]
        for b in range(count):
            rows = taps(blend(parts, fine[b][1]), 16)
            y1[b, x + 1] = dot(w1[...], rows)
    for c in ex:
        c.wait()
    for d, plane, step in ((1, 0, 0), (0, side + 1, 2)):
        a = dot(jnp.concatenate([rx[d, t] for t in range(count)], axis=0), t1[...])
        parts = [a[t * ch : (t + 1) * ch] for t in range(count)]
        for b in range(count):
            rows = taps(blend(parts, fine[b][step]), 16)
            y1[b, plane] = dot(w1[...], rows)
    for b in range(count):
        for x in range(side):
            u = y1[b, x, 0:ch] + y1[b, x + 1, ch : 2 * ch] + y1[b, x + 2, 2 * ch : 3 * ch] + b1
            fst[b, x] = (live[b] * silu(u)).astype(BF16)

    for b in range(count):
        sf[0, b] = fst[b, 0]
        sf[1, b] = fst[b, side - 1]
    pairs = half // 2
    for b in range(count):
        for j in range(pairs):
            for p in (0, 1):
                r0 = ((b * pairs + j) * 2 + p) * ch
                lhs[r0 : r0 + ch, 0:256] = fst[b, 4 * j + p]
                lhs[r0 : r0 + ch, 256:512] = fst[b, 4 * j + 2 + p]
    red[...] = dot(lhs[0 : count * pairs * 2 * ch, :], tred[...]).astype(BF16)
    for b in range(count):
        for j in range(pairs):
            r0 = (b * pairs + j) * 2 * ch
            rows = jnp.concatenate(
                [
                    red[r0 + p * ch : r0 + (p + 1) * ch, k * 128 : (k + 1) * 128]
                    for p in (0, 1)
                    for k in range(4)
                ],
                axis=0,
            )
            v = (live[b] * silu(dot(wr_ref[...], rows) + br)).astype(BF16)
            cin[b, j] = v
            if j == 0:
                sc[0, b] = v
            if j == pairs - 1:
                sc[1, b] = v
    ec, ef = exchange(1, sc, rc), exchange(2, sf, rf)
    for c in ec + ef:
        c.start()

    for x in range(side):
        a = dot(jnp.concatenate([fst[t, x] for t in range(count)], axis=0), t2[...])
        parts = [a[t * ch : (t + 1) * ch] for t in range(count)]
        for b in range(count):
            y1[b, x + 1] = dot(w2f[...], taps(blend(parts, fine[b][1]), 16))

    for j in range(pairs):
        a = dot(jnp.concatenate([cin[t, j] for t in range(count)], axis=0), tc[...])
        parts = [a[t * cc : (t + 1) * cc] for t in range(count)]
        for b in range(count):
            pad[b, j] = blend(parts, mid[b])
    for c in ec:
        c.wait()
    edge = [jnp.where(n1 < 64, rc[0, t].astype(F32), rc[1, t].astype(F32)).astype(BF16) for t in range(count)]
    a = dot(jnp.concatenate(edge, axis=0), tc[...])
    parts = [a[t * cc : (t + 1) * cc] for t in range(count)]
    for b in range(count):
        pad[b, pairs] = blend(parts, rim[b])
    coarse = []
    for b in range(count):
        ys = []
        for j in range(pairs + 1):
            ys.append(dot(wc[...], taps(pad[b, j], 8)))
        y = jnp.concatenate(ys, axis=1)
        width = y.shape[1]
        u = pltpu.roll(y[0:cc], 64, 1) + y[cc : 2 * cc] + pltpu.roll(y[2 * cc :], width - 64, 1) + bc
        co = (valid[b] * silu(u[:, 0 : 64 * half])).astype(BF16)
        coarse.append(co)
        v = (live[b] * (dot(wu_ref[...], co) + bu)).astype(BF16)
        for j in range(pairs):
            up[b, j] = v[:, j * 128 : (j + 1) * 128]
        su[0, b] = v[:, 0:128]
        su[1, b] = v[:, (pairs - 1) * 128 : pairs * 128]
    eu = exchange(3, su, ru)
    for c in eu:
        c.start()

    dense = [dot(co, tbal[...]) for co in coarse]

    def outgoing(r, k):
        total = jnp.zeros_like(dense[0])
        for b in range(count):
            total = total + dense[b] * jnp.where(dest[b] == r * SEND_CAP + k, valid[b], 0.0)
        return total.astype(BF16)

    sent = []
    for d in range(1, n_group):
        other = lax.rem(grp + d, n_group)
        for k in range(SEND_CAP):
            sb[d - 1, k] = outgoing(other, k)
        c = pltpu.make_async_remote_copy(
            src_ref=sb.at[d - 1],
            dst_ref=rb.at[d - 1],
            send_sem=bal_send.at[d - 1],
            recv_sem=bal_recv.at[d - 1],
            device_id={"group": other},
            device_id_type=MESH,
        )
        c.start()
        sent.append(c)
    for k in range(SEND_CAP):
        bal_ref[grp * SEND_CAP + k] = outgoing(grp, k)

    for c in ef:
        c.wait()
    for d, plane, step in ((1, 0, 0), (0, side + 1, 2)):
        a = dot(jnp.concatenate([rf[d, t] for t in range(count)], axis=0), t2[...])
        parts = [a[t * ch : (t + 1) * ch] for t in range(count)]
        for b in range(count):
            y1[b, plane] = dot(w2f[...], taps(blend(parts, fine[b][step]), 16))

    for j in range(pairs):
        a = dot(jnp.concatenate([up[t, j] for t in range(count)], axis=0), tup[...])
        for h in (0, 1):
            parts = [a[t * ch : (t + 1) * ch, h * 256 : (h + 1) * 256] for t in range(count)]
            for b in range(count):
                y2[b, 1 + 2 * j + h] = dot(w2u[...], taps(blend(parts, fine[b][1]), 16))
    for c in eu:
        c.wait()
    for d, plane, step, h in ((1, 0, 0, 1), (0, half + 1, 2, 0)):
        a = dot(jnp.concatenate([ru[d, t] for t in range(count)], axis=0), tup[:, h * 256 : (h + 1) * 256])
        parts = [a[t * ch : (t + 1) * ch] for t in range(count)]
        for b in range(count):
            y2[b, plane] = dot(w2u[...], taps(blend(parts, fine[b][step]), 16))

    for b in range(count):
        done = []
        for x in range(side):
            u = b2
            for p in range(3):
                u = u + y1[b, x + p, p * ch : (p + 1) * ch]
                u = u + y2[b, (x + p + 1) // 2, p * ch : (p + 1) * ch]
            lhs[x * ch : (x + 1) * ch, 0:256] = (live[b] * silu(u)).astype(BF16)
        flat = dot(lhs[0 : side * ch, 0:256], tout[...])
        for x in range(side):
            out_ref[b, :, x * face : (x + 1) * face] = flat[x * ch : (x + 1) * ch].astype(BF16)

    for d, c in enumerate(sent):
        c.wait()
        source = lax.rem(grp + n_group - (d + 1), n_group)
        for k in range(SEND_CAP):
            bal_ref[source * SEND_CAP + k] = rb[d, k]


def local(n_local, n_group, features, neighbours, coarse_dest, *weights):
    count, ch, cells = features.shape
    side = round(cells ** (1 / 3))
    cc = weights[2].shape[0]
    half, face = side // 2, side * side
    pairs = half // 2
    if side + 2 > 16 or half + 2 > 8 or half % 2 or side**3 != cells:
        raise ValueError("side")
    vmem = lambda *shape: pltpu.VMEM(shape, BF16)
    weights = [w.reshape(1, -1) if w.ndim == 1 else w for w in weights]
    whole = pl.BlockSpec(memory_space=pltpu.VMEM)
    smem = pl.BlockSpec(memory_space=pltpu.SMEM)
    return pl.pallas_call(
        functools.partial(kernel, (side, count, ch, cc, n_local, n_group)),
        out_shape=(
            jax.ShapeDtypeStruct(features.shape, BF16),
            jax.ShapeDtypeStruct((n_group * SEND_CAP, cc, half**3), BF16),
        ),
        in_specs=[smem, smem] + [whole] * (1 + len(weights)),
        out_specs=(whole, whole),
        scratch_shapes=[
            vmem(2, count, ch, face),
            vmem(2, count, ch, face),
            vmem(2, count, cc, 128),
            vmem(2, count, cc, 128),
            vmem(2, count, ch, 256),
            vmem(2, count, ch, 256),
            vmem(2, count, ch, 128),
            vmem(2, count, ch, 128),
            vmem(n_group - 1, SEND_CAP, cc, half**3),
            vmem(n_group - 1, SEND_CAP, cc, half**3),
            vmem(face, 256),
            vmem(256, 256),
            vmem(512, 512),
            vmem(128, 128),
            vmem(128, 512),
            vmem(256, face),
            vmem(64 * half, half**3),
            vmem(3 * ch, 9 * ch),
            vmem(3 * cc, 9 * cc),
            vmem(3 * ch, 9 * ch),
            vmem(3 * ch, 9 * ch),
            vmem(side * count * ch, 512),
            vmem(count, pairs + 1, cc, 128),
            pltpu.VMEM((count, side + 2, 3 * ch, 256), F32),
            pltpu.VMEM((count, half + 2, 3 * ch, 256), F32),
            vmem(count, side, ch, 256),
            vmem(count, pairs, cc, 128),
            vmem(count, pairs, ch, 128),
            vmem(count * pairs * 2 * ch, 512),
            pltpu.SemaphoreType.DMA((4, 2)),
            pltpu.SemaphoreType.DMA((4, 2)),
            pltpu.SemaphoreType.DMA((n_group - 1,)),
            pltpu.SemaphoreType.DMA((n_group - 1,)),
        ],
        compiler_params=pltpu.CompilerParams(collective_id=0, has_side_effects=True),
    )(neighbours, coarse_dest, features, *weights)


def solution(mesh):
    slots = P(("group", "local"), None, None)
    return jax.shard_map(
        functools.partial(local, mesh.shape["local"], mesh.shape["group"]),
        mesh=mesh,
        in_specs=(slots, P(("group", "local"), None), P(("group", "local"))) + (P(),) * 10,
        out_specs=(slots, slots),
        check_vma=False,
    )
```

profile of v0, /device:TPU:0, one launch (start us, length us, event | category | flops | bytes accessed | tf_op | source)
XLA Modules:
  0.0 28.9 jit_solution(16136022721900233306)
XLA Ops:
  0.6 25.9 %shard_map.140 = (bf16[2,32,1728]{2,1,0:T(8,128)(2,1)}, bf16[4,64,216]{2,1,0:T(8,128)(2,1)}) custom-call(s32[2,27]{1,0:T(2,128)} %nb.1, s32[2]{0:T(128)} %dest.1, bf16[2,32,1728]{2,1,0:T(8,128)(2,1)} %x_ref.1, bf16[32,864]{1,0:T(8,128)(2,1)} %w1_ref.1, f32[1,32]{1,0:T(1,128)} %bitcast.5, bf16[64,256]{1,0:T(8,128)(2,1)} %wr_ref.1, f32[1,64]{1,0:T(1,128)} %bitcast.6, ...), custom_call_target="tpu_custom_call" | custom-call | tf_op jit(solution)/shard_map/pallas_call | solution.py:389
  26.5 0.0 copy-start
  26.5 1.7 %copy.17 = bf16[2,32,1728]{2,1,0:T(8,128)(2,1)} copy(bf16[2,32,1728]{2,1,0:T(8,128)(2,1)} %get-tuple-element.4) | data formatting | bytes 442368
  28.2 0.0 copy-done
  28.2 0.7 %copy.18 = bf16[4,64,216]{2,1,0:T(8,128)(2,1)} copy(bf16[4,64,216]{2,1,0:T(8,128)(2,1)S(1)} %copy-done) | data formatting | bytes 221184
Async XLA Ops:
  26.5 1.7 %copy-start = (bf16[4,64,216]{2,1,0:T(8,128)(2,1)S(1)}, bf16[4,64,216]{2,1,0:T(8,128)(2,1)}, u32[]{:S(2)}) copy-start(bf16[4,64,216]{2,1,0:T(8,128)(2,1)} %get-tuple-element.5) | copy-start | bytes 331780
where the time goes:
time: 29 us; the launch traced here: 28.9 us
  Pallas kernels  25.9 us (89%)
  local copies, waits for them, and re-layouts  2.34 us (8%)
  between operations  0.65 us (2%)
    pallas_call x1, Pallas kernels, local(): pl.pallas_call(functools.partial(kernel, (side, count, ch, cc, n_local, n...  25.9 us
    unnamed x4, local copies, waits for them, and re-layouts  2.34 us

commit v1 on v0

--- a/solution.py
+++ b/solution.py
@@ -88,6 +88,9 @@
     cin,
     up,
     red,
+    sel,
+    fm,
+    cm,
     send_sem,
     recv_sem,
     bal_send,
@@ -101,6 +104,8 @@
     grp = lax.axis_index("group")
     right, left = lax.rem(me + 1, n_local), lax.rem(me + n_local - 1, n_local)
     ends = (left, right)
+    has_left, has_right = me > 0, me < n_local - 1
+    sends, receives = (has_left, has_right), (has_right, has_left)
 
     def exchange(e, src, dst):
         copies = []
@@ -117,9 +122,32 @@
             )
         return copies
 
+    def start(copies):
+        for d in (0, 1):
+            pl.when(sends[d])(copies[d].start)
+
+    def receive(copies):
+        for d in (0, 1):
+            pl.when(receives[d])(copies[d].wait_recv)
+
+    def finish(copies):
+        for d in (0, 1):
+            pl.when(sends[d])(copies[d].wait_send)
+
+    for d in (0, 1):
+
+        @pl.when(jnp.logical_not(receives[d]))
+        def _():
+            for buf in (rx, rc, rf, ru):
+                buf[d] = jnp.zeros(buf.shape[1:], BF16)
+
     barrier = pltpu.get_barrier_semaphore()
-    for e in ends:
-        pl.semaphore_signal(barrier, inc=1, device_id={"local": e}, device_id_type=MESH)
+    for d in (0, 1):
+
+        @pl.when(sends[d])
+        def _():
+            pl.semaphore_signal(barrier, inc=1, device_id={"local": ends[d]}, device_id_type=MESH)
+
     for d in range(1, n_group):
         pl.semaphore_signal(
             barrier, inc=1, device_id={"group": lax.rem(grp + d, n_group)}, device_id_type=MESH
@@ -127,11 +155,6 @@
     for t in range(count):
         sx[0, t] = x_ref[t, :, 0:face]
         sx[1, t] = x_ref[t, :, (side - 1) * face : side * face]
-    pl.semaphore_wait(barrier, 2 + n_group - 1)
-    ex = exchange(0, sx, rx)
-    for c in ex:
-        c.start()
-
     n = iota((1, 256), 1)
     ny, nz = n >> 4, n & 15
     py = jnp.where(ny == 0, side - 1, jnp.where(ny == side + 1, 0, ny - 1))
@@ -205,11 +228,18 @@
         for b in range(count)
     ]
 
+    for b in range(count):
+        for t in range(count):
+            for s in range(3):
+                fm[b, s, t] = jnp.broadcast_to(fine[b][s][t], (ch, 256)).astype(BF16)
+            cm[b, 0, t] = jnp.broadcast_to(mid[b][t], (cc, 128)).astype(BF16)
+            cm[b, 1, t] = jnp.broadcast_to(rim[b][t], (cc, 128)).astype(BF16)
+
     def blend(parts, masks):
         total = parts[0] * masks[0]
-        for part, mask in zip(parts[1:], masks[1:]):
-            total = total + part * mask
-        return total.astype(BF16)
+        for t in range(1, count):
+            total = total + parts[t] * masks[t]
+        return total
 
     def taps(v, stride):
         return jnp.concatenate([shifted(v, q * stride + r) for q in range(3) for r in range(3)], axis=0)
@@ -219,19 +249,22 @@
             lhs[(x * count + t) * ch : (x * count + t + 1) * ch, 0:face] = x_ref[
                 t, :, x * face : (x + 1) * face
             ]
+    beside = jnp.where(has_left, 1, 0) + jnp.where(has_right, 1, 0)
+    pl.semaphore_wait(barrier, beside + n_group - 1)
+    ex = exchange(0, sx, rx)
+    start(ex)
+    sel[...] = dot(lhs[:, 0:face], t1[...]).astype(BF16)
     for x in range(side):
-        a = dot(lhs[x * count * ch : (x + 1) * count * ch, 0:face], t1[...])
+        parts = [sel[(x * count + t) * ch : (x * count + t + 1) * ch] for t in range(count)]
+        for b in range(count):
+            rows = taps(blend(parts, fm.at[b, 1]), 16)
+            y1[b, x + 1] = dot(w1[...], rows)
+    receive(ex)
+    for d, plane, step in ((1, 0, 0), (0, side + 1, 2)):
+        a = dot(jnp.concatenate([rx[d, t] for t in range(count)], axis=0), t1[...]).astype(BF16)
         parts = [a[t * ch : (t + 1) * ch] for t in range(count)]
         for b in range(count):
-            rows = taps(blend(parts, fine[b][1]), 16)
-            y1[b, x + 1] = dot(w1[...], rows)
-    for c in ex:
-        c.wait()
-    for d, plane, step in ((1, 0, 0), (0, side + 1, 2)):
-        a = dot(jnp.concatenate([rx[d, t] for t in range(count)], axis=0), t1[...])
-        parts = [a[t * ch : (t + 1) * ch] for t in range(count)]
-        for b in range(count):
-            rows = taps(blend(parts, fine[b][step]), 16)
+            rows = taps(blend(parts, fm.at[b, step]), 16)
             y1[b, plane] = dot(w1[...], rows)
     for b in range(count):
         for x in range(side):
@@ -267,27 +300,29 @@
             if j == pairs - 1:
                 sc[1, b] = v
     ec, ef = exchange(1, sc, rc), exchange(2, sf, rf)
-    for c in ec + ef:
-        c.start()
-
+    start(ec)
+    start(ef)
+
+    for t in range(count):
+        for x in range(side):
+            lhs[(x * count + t) * ch : (x * count + t + 1) * ch, 0:256] = fst[t, x]
+    sel[...] = dot(lhs[:, 0:256], t2[...]).astype(BF16)
     for x in range(side):
-        a = dot(jnp.concatenate([fst[t, x] for t in range(count)], axis=0), t2[...])
-        parts = [a[t * ch : (t + 1) * ch] for t in range(count)]
-        for b in range(count):
-            y1[b, x + 1] = dot(w2f[...], taps(blend(parts, fine[b][1]), 16))
+        parts = [sel[(x * count + t) * ch : (x * count + t + 1) * ch] for t in range(count)]
+        for b in range(count):
+            y1[b, x + 1] = dot(w2f[...], taps(blend(parts, fm.at[b, 1]), 16))
 
     for j in range(pairs):
-        a = dot(jnp.concatenate([cin[t, j] for t in range(count)], axis=0), tc[...])
+        a = dot(jnp.concatenate([cin[t, j] for t in range(count)], axis=0), tc[...]).astype(BF16)
         parts = [a[t * cc : (t + 1) * cc] for t in range(count)]
         for b in range(count):
-            pad[b, j] = blend(parts, mid[b])
-    for c in ec:
-        c.wait()
+            pad[b, j] = blend(parts, cm.at[b, 0])
+    receive(ec)
     edge = [jnp.where(n1 < 64, rc[0, t].astype(F32), rc[1, t].astype(F32)).astype(BF16) for t in range(count)]
-    a = dot(jnp.concatenate(edge, axis=0), tc[...])
+    a = dot(jnp.concatenate(edge, axis=0), tc[...]).astype(BF16)
     parts = [a[t * cc : (t + 1) * cc] for t in range(count)]
     for b in range(count):
-        pad[b, pairs] = blend(parts, rim[b])
+        pad[b, pairs] = blend(parts, cm.at[b, 1])
     coarse = []
     for b in range(count):
         ys = []
@@ -304,8 +339,7 @@
         su[0, b] = v[:, 0:128]
         su[1, b] = v[:, (pairs - 1) * 128 : pairs * 128]
     eu = exchange(3, su, ru)
-    for c in eu:
-        c.start()
+    start(eu)
 
     dense = [dot(co, tbal[...]) for co in coarse]
 
@@ -333,27 +367,25 @@
     for k in range(SEND_CAP):
         bal_ref[grp * SEND_CAP + k] = outgoing(grp, k)
 
-    for c in ef:
-        c.wait()
+    receive(ef)
     for d, plane, step in ((1, 0, 0), (0, side + 1, 2)):
-        a = dot(jnp.concatenate([rf[d, t] for t in range(count)], axis=0), t2[...])
+        a = dot(jnp.concatenate([rf[d, t] for t in range(count)], axis=0), t2[...]).astype(BF16)
         parts = [a[t * ch : (t + 1) * ch] for t in range(count)]
         for b in range(count):
-            y1[b, plane] = dot(w2f[...], taps(blend(parts, fine[b][step]), 16))
+            y1[b, plane] = dot(w2f[...], taps(blend(parts, fm.at[b, step]), 16))
 
     for j in range(pairs):
-        a = dot(jnp.concatenate([up[t, j] for t in range(count)], axis=0), tup[...])
+        a = dot(jnp.concatenate([up[t, j] for t in range(count)], axis=0), tup[...]).astype(BF16)
         for h in (0, 1):
             parts = [a[t * ch : (t + 1) * ch, h * 256 : (h + 1) * 256] for t in range(count)]
             for b in range(count):
-                y2[b, 1 + 2 * j + h] = dot(w2u[...], taps(blend(parts, fine[b][1]), 16))
-    for c in eu:
-        c.wait()
+                y2[b, 1 + 2 * j + h] = dot(w2u[...], taps(blend(parts, fm.at[b, 1]), 16))
+    receive(eu)
     for d, plane, step, h in ((1, 0, 0, 1), (0, half + 1, 2, 0)):
-        a = dot(jnp.concatenate([ru[d, t] for t in range(count)], axis=0), tup[:, h * 256 : (h + 1) * 256])
+        a = dot(jnp.concatenate([ru[d, t] for t in range(count)], axis=0), tup[:, h * 256 : (h + 1) * 256]).astype(BF16)
         parts = [a[t * ch : (t + 1) * ch] for t in range(count)]
         for b in range(count):
-            y2[b, plane] = dot(w2u[...], taps(blend(parts, fine[b][step]), 16))
+            y2[b, plane] = dot(w2u[...], taps(blend(parts, fm.at[b, step]), 16))
 
     for b in range(count):
         done = []
@@ -367,6 +399,8 @@
         for x in range(side):
             out_ref[b, :, x * face : (x + 1) * face] = flat[x * ch : (x + 1) * ch].astype(BF16)
 
+    for copies in (ex, ec, ef, eu):
+        finish(copies)
     for d, c in enumerate(sent):
         c.wait()
         source = lax.rem(grp + n_group - (d + 1), n_group)
@@ -424,6 +458,9 @@
             vmem(count, pairs, cc, 128),
             vmem(count, pairs, ch, 128),
             vmem(count * pairs * 2 * ch, 512),
+            vmem(side * count * ch, 256),
+            vmem(count, 3, count, ch, 256),
+            vmem(count, 2, count, cc, 128),
             pltpu.SemaphoreType.DMA((4, 2)),
             pltpu.SemaphoreType.DMA((4, 2)),
             pltpu.SemaphoreType.DMA((n_group - 1,)),

time: 29 us -> 22.1 us (0.76)
  Pallas kernels: 25.9 us -> 18.9 us
    pallas_call x1, Pallas kernels: 25.9 us -> 18.9 us  [local(): pl.pallas_call(functools.partial(kernel, (side, count, ch, cc, n_local, n...]
where the time goes in v1:
time: 22.1 us; the launch traced here: 21.9 us
  Pallas kernels  18.9 us (86%)
  local copies, waits for them, and re-layouts  2.34 us (11%)
  between operations  0.65 us (3%)
    pallas_call x1, Pallas kernels, local(): pl.pallas_call(functools.partial(kernel, (side, count, ch, cc, n_local, n...  18.9 us
    unnamed x4, local copies, waits for them, and re-layouts  2.34 us

profile of v1, /device:TPU:0, one launch (start us, length us, event | category | flops | bytes accessed | tf_op | source)
XLA Modules:
  0.0 21.9 jit_solution(15518479650050657754)
XLA Ops:
  0.6 18.9 %shard_map.140 = (bf16[2,32,1728]{2,1,0:T(8,128)(2,1)}, bf16[4,64,216]{2,1,0:T(8,128)(2,1)}) custom-call(s32[2,27]{1,0:T(2,128)} %nb.1, s32[2]{0:T(128)} %dest.1, bf16[2,32,1728]{2,1,0:T(8,128)(2,1)} %x_ref.1, bf16[32,864]{1,0:T(8,128)(2,1)} %w1_ref.1, f32[1,32]{1,0:T(1,128)} %bitcast.5, bf16[64,256]{1,0:T(8,128)(2,1)} %wr_ref.1, f32[1,64]{1,0:T(1,128)} %bitcast.6, ...), custom_call_target="tpu_custom_call" | custom-call | tf_op jit(solution)/shard_map/pallas_call | solution.py:423
  19.6 0.0 copy-start
  19.6 1.7 %copy.17 = bf16[2,32,1728]{2,1,0:T(8,128)(2,1)} copy(bf16[2,32,1728]{2,1,0:T(8,128)(2,1)} %get-tuple-element.4) | data formatting | bytes 442368
  21.3 0.0 copy-done
  21.3 0.7 %copy.18 = bf16[4,64,216]{2,1,0:T(8,128)(2,1)} copy(bf16[4,64,216]{2,1,0:T(8,128)(2,1)S(1)} %copy-done) | data formatting | bytes 221184
Async XLA Ops:
  19.6 1.7 %copy-start = (bf16[4,64,216]{2,1,0:T(8,128)(2,1)S(1)}, bf16[4,64,216]{2,1,0:T(8,128)(2,1)}, u32[]{:S(2)}) copy-start(bf16[4,64,216]{2,1,0:T(8,128)(2,1)} %get-tuple-element.5) | copy-start | bytes 331780

commit v2 on v1

--- a/solution.py
+++ b/solution.py
@@ -244,6 +244,12 @@
     def taps(v, stride):
         return jnp.concatenate([shifted(v, q * stride + r) for q in range(3) for r in range(3)], axis=0)
 
+    def convolve(dst, plane, weight, parts, step):
+        both = [taps(blend(parts, fm.at[b, step]), 16) for b in range(count)]
+        y = dot(weight[...], jnp.concatenate(both, axis=1))
+        for b in range(count):
+            dst[b, plane] = y[:, b * 256 : (b + 1) * 256]
+
     for t in range(count):
         for x in range(side):
             lhs[(x * count + t) * ch : (x * count + t + 1) * ch, 0:face] = x_ref[
@@ -256,16 +262,12 @@
     sel[...] = dot(lhs[:, 0:face], t1[...]).astype(BF16)
     for x in range(side):
         parts = [sel[(x * count + t) * ch : (x * count + t + 1) * ch] for t in range(count)]
-        for b in range(count):
-            rows = taps(blend(parts, fm.at[b, 1]), 16)
-            y1[b, x + 1] = dot(w1[...], rows)
+        convolve(y1, x + 1, w1, parts, 1)
     receive(ex)
     for d, plane, step in ((1, 0, 0), (0, side + 1, 2)):
         a = dot(jnp.concatenate([rx[d, t] for t in range(count)], axis=0), t1[...]).astype(BF16)
         parts = [a[t * ch : (t + 1) * ch] for t in range(count)]
-        for b in range(count):
-            rows = taps(blend(parts, fm.at[b, step]), 16)
-            y1[b, plane] = dot(w1[...], rows)
+        convolve(y1, plane, w1, parts, step)
     for b in range(count):
         for x in range(side):
             u = y1[b, x, 0:ch] + y1[b, x + 1, ch : 2 * ch] + y1[b, x + 2, 2 * ch : 3 * ch] + b1
@@ -309,8 +311,7 @@
     sel[...] = dot(lhs[:, 0:256], t2[...]).astype(BF16)
     for x in range(side):
         parts = [sel[(x * count + t) * ch : (x * count + t + 1) * ch] for t in range(count)]
-        for b in range(count):
-            y1[b, x + 1] = dot(w2f[...], taps(blend(parts, fm.at[b, 1]), 16))
+        convolve(y1, x + 1, w2f, parts, 1)
 
     for j in range(pairs):
         a = dot(jnp.concatenate([cin[t, j] for t in range(count)], axis=0), tc[...]).astype(BF16)
@@ -325,10 +326,7 @@
         pad[b, pairs] = blend(parts, cm.at[b, 1])
     coarse = []
     for b in range(count):
-        ys = []
-        for j in range(pairs + 1):
-            ys.append(dot(wc[...], taps(pad[b, j], 8)))
-        y = jnp.concatenate(ys, axis=1)
+        y = dot(wc[...], jnp.concatenate([taps(pad[b, j], 8) for j in range(pairs + 1)], axis=1))
         width = y.shape[1]
         u = pltpu.roll(y[0:cc], 64, 1) + y[cc : 2 * cc] + pltpu.roll(y[2 * cc :], width - 64, 1) + bc
         co = (valid[b] * silu(u[:, 0 : 64 * half])).astype(BF16)
@@ -371,21 +369,18 @@
     for d, plane, step in ((1, 0, 0), (0, side + 1, 2)):
         a = dot(jnp.concatenate([rf[d, t] for t in range(count)], axis=0), t2[...]).astype(BF16)
         parts = [a[t * ch : (t + 1) * ch] for t in range(count)]
-        for b in range(count):
-            y1[b, plane] = dot(w2f[...], taps(blend(parts, fm.at[b, step]), 16))
+        convolve(y1, plane, w2f, parts, step)
 
     for j in range(pairs):
         a = dot(jnp.concatenate([up[t, j] for t in range(count)], axis=0), tup[...]).astype(BF16)
         for h in (0, 1):
             parts = [a[t * ch : (t + 1) * ch, h * 256 : (h + 1) * 256] for t in range(count)]
-            for b in range(count):
-                y2[b, 1 + 2 * j + h] = dot(w2u[...], taps(blend(parts, fm.at[b, 1]), 16))
+            convolve(y2, 1 + 2 * j + h, w2u, parts, 1)
     receive(eu)
     for d, plane, step, h in ((1, 0, 0, 1), (0, half + 1, 2, 0)):
         a = dot(jnp.concatenate([ru[d, t] for t in range(count)], axis=0), tup[:, h * 256 : (h + 1) * 256]).astype(BF16)
         parts = [a[t * ch : (t + 1) * ch] for t in range(count)]
-        for b in range(count):
-            y2[b, plane] = dot(w2u[...], taps(blend(parts, fm.at[b, step]), 16))
+        convolve(y2, plane, w2u, parts, step)
 
     for b in range(count):
         done = []

time: 22.1 us -> 21.9 us (level)
  no operation moved by 1% of the time
where the time goes in v2:
time: 21.9 us; the launch traced here: 21.7 us
  Pallas kernels  18.7 us (85%)
  local copies, waits for them, and re-layouts  2.34 us (11%)
  between operations  0.65 us (3%)
    pallas_call x1, Pallas kernels, local(): pl.pallas_call(functools.partial(kernel, (side, count, ch, cc, n_local, n...  18.7 us
    unnamed x4, local copies, waits for them, and re-layouts  2.34 us

profile of v2, /device:TPU:0, one launch (start us, length us, event | category | flops | bytes accessed | tf_op | source)
XLA Modules:
  0.0 21.7 jit_solution(17009095326585506277)
XLA Ops:
  0.6 18.7 %shard_map.140 = (bf16[2,32,1728]{2,1,0:T(8,128)(2,1)}, bf16[4,64,216]{2,1,0:T(8,128)(2,1)}) custom-call(s32[2,27]{1,0:T(2,128)} %nb.1, s32[2]{0:T(128)} %dest.1, bf16[2,32,1728]{2,1,0:T(8,128)(2,1)} %x_ref.1, bf16[32,864]{1,0:T(8,128)(2,1)} %w1_ref.1, f32[1,32]{1,0:T(1,128)} %bitcast.5, bf16[64,256]{1,0:T(8,128)(2,1)} %wr_ref.1, f32[1,64]{1,0:T(1,128)} %bitcast.6, ...), custom_call_target="tpu_custom_call" | custom-call | tf_op jit(solution)/shard_map/pallas_call | solution.py:418
  19.4 0.0 copy-start
  19.4 1.7 %copy.17 = bf16[2,32,1728]{2,1,0:T(8,128)(2,1)} copy(bf16[2,32,1728]{2,1,0:T(8,128)(2,1)} %get-tuple-element.4) | data formatting | bytes 442368
  21.1 0.0 copy-done
  21.1 0.7 %copy.18 = bf16[4,64,216]{2,1,0:T(8,128)(2,1)} copy(bf16[4,64,216]{2,1,0:T(8,128)(2,1)S(1)} %copy-done) | data formatting | bytes 221184
Async XLA Ops:
  19.4 1.7 %copy-start = (bf16[4,64,216]{2,1,0:T(8,128)(2,1)S(1)}, bf16[4,64,216]{2,1,0:T(8,128)(2,1)}, u32[]{:S(2)}) copy-start(bf16[4,64,216]{2,1,0:T(8,128)(2,1)} %get-tuple-element.5) | copy-start | bytes 331780
